TPU v7x, 256 devices: a whole 4x4x8 slice. The times are simulated.
256 devices in a mesh: dp: 16 (over x, y_hi, core), ctx: 16 (over z, y_lo).
Axes of the slice: x: 4, y: 4 (y_hi: 2, y_lo: 2; y = y_hi * 2 + y_lo), z: 8, core: 2. Of those that a mesh axis runs over, the one named last changes fastest.
Arguments:
- query_frames: bfloat16 [65536, 2560], P(('dp', 'ctx')), parts along dimension 0, may hold values from -8 to 8
- key_frames: bfloat16 [65536, 2560], P(('dp', 'ctx')), parts along dimension 0, may hold values from -8 to 8
- value_frames: bfloat16 [65536, 2560], P(('dp', 'ctx')), parts along dimension 0, may hold values from -6 to 6
- stream: bfloat16 [65536, 5120], P(('dp', 'ctx')), parts along dimension 0, may hold values from -1.25 to 1.25
- out_weight: bfloat16 [2560, 5120], P('ctx'), may hold values from -0.125 to 0.125
Outputs:
- layer_out: bfloat16 [65536, 5120], P(('dp', 'ctx')), parts along dimension 0
There are 16 independent parts, one for each index of `dp`. A program takes and returns all parts, laid end to end along the dimension named above; an argument that names none is the same for every part. Nothing has to cross between parts.
All inputs are finite; a program needn't handle non-finite values.
Results may differ from a plain program's by a relative error of at most 0.01.
Values may be sent and summed in bfloat16 or wider, within the bound.
A program may use at most 128 MiB of HBM per device.

v0:
```python
import jax
import jax.numpy as jnp
from jax import lax
from jax.sharding import PartitionSpec as P

HEADS = 20
HEAD_SIZE = 128


def passed_along(value, axis, steps):
    count = lax.axis_size(axis)
    leading, last = (max(0, -steps), min(count, count - steps))
    return lax.ppermute(value, axis, [(source, source + steps) for source in range(leading, last)])


def attend_window(query_block, key_window, value_window, valid):
    block_rows = query_block.shape[0]
    window_rows = key_window.shape[0]
    query_heads = query_block.reshape(block_rows, HEADS, HEAD_SIZE)
    key_heads = key_window.reshape(window_rows, HEADS, HEAD_SIZE)
    value_heads = value_window.reshape(window_rows, HEADS, HEAD_SIZE)
    scores = jnp.einsum(
        "qhd,khd->hqk", query_heads, key_heads, preferred_element_type=jnp.float32
    ) * HEAD_SIZE ** (-0.5)
    scores = jnp.where(valid[None, None, :], scores, -1e30)
    largest = jnp.max(scores, axis=2, keepdims=True)
    expon = jnp.exp(scores - largest)
    probs = (expon / jnp.sum(expon, axis=2, keepdims=True)).astype(jnp.bfloat16)
    context = jnp.einsum("hqk,khd->qhd", probs, value_heads, preferred_element_type=jnp.float32)
    return context.astype(jnp.bfloat16).reshape(block_rows, HEADS * HEAD_SIZE)


def local(query_frames, key_frames, value_frames, stream, out_weight):
    block_rows = query_frames.shape[0]
    position = lax.axis_index("ctx")
    members = lax.axis_size("ctx")
    key_value = jnp.stack([key_frames, value_frames], 0)
    earlier = passed_along(key_value, "ctx", 1)
    later = passed_along(key_value, "ctx", -1)
    window = jnp.concatenate([earlier, key_value, later], 1)
    earlier_ok = jnp.broadcast_to(position > 0, (block_rows,))
    middle_ok = jnp.ones((block_rows,), dtype=bool)
    later_ok = jnp.broadcast_to(position < members - 1, (block_rows,))
    valid = jnp.concatenate([earlier_ok, middle_ok, later_ok])
    context = attend_window(query_frames, window[0], window[1], valid)
    product = jnp.dot(
        context,
        lax.all_gather(out_weight, "ctx", axis=0, tiled=True),
        preferred_element_type=jnp.float32,
    )
    return (stream.astype(jnp.float32) + product).astype(jnp.bfloat16)


def solution(mesh):
    in_specs = (
        P(("dp", "ctx"), None),
        P(("dp", "ctx"), None),
        P(("dp", "ctx"), None),
        P(("dp", "ctx"), None),
        P("ctx", None),
    )
    out_specs = P(("dp", "ctx"), None)
    return jax.shard_map(local, mesh=mesh, in_specs=in_specs, out_specs=out_specs, check_vma=False)
```

profile of v0, /device:TPU:151, one launch (start us, length us, event | category | flops | bytes accessed | tf_op | source)
XLA Modules:
  0.0 679.2 jit_solution(7607029471892932784)
XLA Ops:
  6.5 0.0 all-gather.2.cloned.1.call-start
  6.5 0.7 all-gather.2.cloned.1.call-update
  7.3 1.6 copy.9
  8.9 1.6 copy.10
  10.5 1.7 pad_maximum_fusion.1
  12.2 2.9 collective-permute-start
  15.1 4.5 collective-permute-start.1
  19.6 2.4 copy.11
  22.1 226.5 %collective-permute-done = bf16[2,256,2560]{1,2,0:T(8,128)(2,1)} collective-permute-done((bf16[2,256,2560]{1,2,0:T(8,128)(2,1)}, bf16[2,256,2560]{1,2,0:T(8,128)(2,1)}, u32[]{:S(2)}, u32[]{:S(2)}) %collective-permute-start) | collective-permute-done | bytes 2621472 | tf_op jit(solution)/shard_map/ppermute | solution.py:13
  248.5 9.1 %collective-permute-done.1 = bf16[2,256,2560]{1,2,0:T(8,128)(2,1)} collective-permute-done((bf16[2,256,2560]{1,2,0:T(8,128)(2,1)}, bf16[2,256,2560]{1,2,0:T(8,128)(2,1)}, u32[]{:S(2)}, u32[]{:S(2)}) %collective-permute-start.1) | collective-permute-done | bytes 2621472 | tf_op jit(solution)/shard_map/ppermute | solution.py:13
  257.7 3.4 pad_maximum_fusion
  261.0 0.0 copy-start.1
  261.1 3.3 fusion.15
  264.4 0.0 copy-done.1
  264.4 10.6 %fusion.16 = (f32[20,256]{1,0:T(8,128)S(1)}, f32[20,256,768]{1,2,0:T(8,128)}) fusion(pred[768]{0:T(1024)(128)(4,1)S(1)} %pad_add_fusion, bf16[768,20,128]{0,2,1:T(8,128)(2,1)} %bitcast.31, bf16[256,20,128]{0,2,1:T(8,128)(2,1)S(1)} %bitcast.33), kind=kOutput, calls=%fused_computation.21 | convolution fusion | flops 1022362368 | bytes 20992768 | tf_op jit(solution)/shard_map/sub | solution.py:27
  275.0 0.0 copy-start
  275.0 9.2 %fusion.10 = bf16[20,128,256]{2,1,0:T(8,128)(2,1)} fusion(bf16[768,20,128]{0,2,1:T(8,128)(2,1)} %bitcast.30, f32[20,256,768]{1,2,0:T(8,128)} %get-tuple-element.8, f32[20,256]{1,0:T(8,128)S(1)} %get-tuple-element.7), kind=kOutput, calls=%fused_computation.15 | convolution fusion | flops 1015152640 | bytes 20992000 | tf_op jit(solution)/shard_map/hqk,khd->qhd/dot_general | solution.py:29
  284.2 374.7 %all-gather.2.cloned.1.call-done = bf16[2560,5120]{1,0:T(8,128)(2,1)} async-done(((bf16[160,5120]{1,0:T(8,128)(2,1)}), bf16[2560,5120]{1,0:T(8,128)(2,1)}) %all-gather.2.cloned.1.call-update) | async-done | bytes 26214416 | tf_op jit(solution)/shard_map/all_gather | solution.py:48
  658.9 0.0 copy-done
  658.9 13.5 %fusion.9 = bf16[256,5120]{1,0:T(8,128)(2,1)} fusion(bf16[256,2560]{0,1:T(8,128)(2,1)} %bitcast.32, bf16[2560,5120]{1,0:T(8,128)(2,1)} %all-gather.2.cloned.1.call-done, bf16[256,5120]{1,0:T(8,128)(2,1)S(1)} %copy-done), kind=kOutput, calls=%fused_computation.13 | convolution fusion | flops 6714818560 | bytes 32768000 | tf_op jit(solution)/shard_map/dot_general | solution.py:46
  (4 shorter events, 0.0 us)
Async XLA Ops:
  6.5 652.3 %all-gather.2.cloned.1.call-start = ((), (), s32[]{:S(2)}) async-start(), calls=%async_computation | async-start | bytes 27852800 | tf_op jit(solution)/shard_map/all_gather | solution.py:48
  12.2 236.4 %collective-permute-start = (bf16[2,256,2560]{1,2,0:T(8,128)(2,1)}, bf16[2,256,2560]{1,2,0:T(8,128)(2,1)}, u32[]{:S(2)}, u32[]{:S(2)}) collective-permute-start(bf16[2,256,2560]{1,2,0:T(8,128)(2,1)} %pad_maximum_fusion.1), channel_id=1, source_target_pairs={{0,1},{1,2},{2,3},{3,4},{4,5},{5,6},{6,7},{7,8},{8,9},{9,10},{10,1... | collective-permute-start | bytes 7864328 | tf_op jit(solution)/shard_map/ppermute | solution.py:13
  15.1 242.6 %collective-permute-start.1 = (bf16[2,256,2560]{1,2,0:T(8,128)(2,1)}, bf16[2,256,2560]{1,2,0:T(8,128)(2,1)}, u32[]{:S(2)}, u32[]{:S(2)}) collective-permute-start(bf16[2,256,2560]{1,2,0:T(8,128)(2,1)} %pad_maximum_fusion.1), channel_id=1, source_target_pairs={{1,0},{2,1},{3,2},{4,3},{5,4},{6,5},{7,6},{8,7},{9,8},{10,9},{11,1... | collective-permute-start | bytes 7864328 | tf_op jit(solution)/shard_map/ppermute | solution.py:13
  261.0 3.3 copy-start.1
  275.0 383.9 %copy-start = (bf16[256,5120]{1,0:T(8,128)(2,1)S(1)}, bf16[256,5120]{1,0:T(8,128)(2,1)}, u32[]{:S(2)}) copy-start(bf16[256,5120]{1,0:T(8,128)(2,1)} %param.8) | copy-start | bytes 7864324
Sparse Core Ops, SparseCore 0:
  9.1 649.7 all-gather.1
where the time goes:
time: 679 us
  waiting for transfers between devices  611 us (90%)
  matrix products  33.3 us (5%)
  between operations  13.5 us (2%)
  local copies, waits for them, and re-layouts  8.97 us (1%)
  starting transfers between devices  7.39 us (1%)
    all_gather x1, waiting for transfers between devices, local(): lax.all_gather(out_weight, 'ctx', axis=0, tiled=True)  375 us
    ppermute x2, waiting for transfers between devices, passed_along(): lax.ppermute(value, axis, [(source, source + steps) for source in range(l...  236 us
  transfers between devices with their start and end apart: 3, of which 3 were waited for; matrix products, arithmetic and copies ran while one was open for 5% of the time, Pallas kernels for 0%

commit v1 on v0

--- a/solution.py
+++ b/solution.py
@@ -5,6 +5,9 @@
 
 HEADS = 20
 HEAD_SIZE = 128
+perform_ports = lambda local_values: jnp.concatenate(
+    lax.all_to_all(jnp.stack(lax.axis_size("ctx") * [local_values], axis=0), "ctx", 0, 0), 0
+)
 
 
 def passed_along(value, axis, steps):
@@ -43,11 +46,7 @@
     later_ok = jnp.broadcast_to(position < members - 1, (block_rows,))
     valid = jnp.concatenate([earlier_ok, middle_ok, later_ok])
     context = attend_window(query_frames, window[0], window[1], valid)
-    product = jnp.dot(
-        context,
-        lax.all_gather(out_weight, "ctx", axis=0, tiled=True),
-        preferred_element_type=jnp.float32,
-    )
+    product = jnp.dot(context, perform_ports(out_weight), preferred_element_type=jnp.float32)
     return (stream.astype(jnp.float32) + product).astype(jnp.bfloat16)
 
 

time: 679 us -> 719 us (1.059)
  the two profiles are of different devices: /device:TPU:151 before, /device:TPU:162 now
where the time goes in v1:
time: 719 us
  waiting for transfers between devices  648 us (90%)
  matrix products  33.3 us (5%)
  local copies, waits for them, and re-layouts  17.8 us (2%)
  starting transfers between devices  14.1 us (2%)
    ppermute x2, waiting for transfers between devices, passed_along(): lax.ppermute(value, axis, [(source, source + steps) for source in range(l...  648 us
  transfers between devices with their start and end apart: 3, of which 2 were waited for; matrix products, arithmetic and copies ran while one was open for 5% of the time, Pallas kernels for 0%

profile of v1, /device:TPU:162, one launch (start us, length us, event | category | flops | bytes accessed | tf_op | source)
XLA Modules:
  0.0 718.6 jit_solution(11127357772661774270)
XLA Ops:
  0.0 9.7 %stack.11 = bf16[16,160,5120]{2,1,0:T(8,128)(2,1)} broadcast(bf16[160,5120]{1,0:T(8,128)(2,1)} %param.9), dimensions={1,2} | broadcast | bytes 27852800 | tf_op jit(solution)/shard_map/stack | solution.py:9
  9.7 0.0 copy-start.1
  9.7 7.9 %all-to-all-start = ((bf16[16,160,5120]{2,1,0:T(8,128)(2,1)}), bf16[16,160,5120]{2,1,0:T(8,128)(2,1)}, u32[]{:S(2)}, u32[]{:S(2)}) async-start(bf16[16,160,5120]{2,1,0:T(8,128)(2,1)} %stack.11), calls=%async_computation | async-start | bytes 52428800 | tf_op jit(solution)/shard_map/all_to_all | solution.py:9
  17.6 0.0 copy-done.1
  17.6 0.6 copy.9
  18.2 1.6 copy.10
  19.8 1.7 pad_maximum_fusion.1
  21.6 4.3 collective-permute-start.1
  25.8 1.9 collective-permute-start
  27.8 2.5 copy.11
  30.3 625.2 %collective-permute-done.1 = bf16[2,256,2560]{1,2,0:T(8,128)(2,1)} collective-permute-done((bf16[2,256,2560]{1,2,0:T(8,128)(2,1)}, bf16[2,256,2560]{1,2,0:T(8,128)(2,1)}, u32[]{:S(2)}, u32[]{:S(2)}) %collective-permute-start.1) | collective-permute-done | bytes 2621472 | tf_op jit(solution)/shard_map/ppermute | solution.py:16
  655.4 23.1 %collective-permute-done = bf16[2,256,2560]{1,2,0:T(8,128)(2,1)} collective-permute-done((bf16[2,256,2560]{1,2,0:T(8,128)(2,1)}, bf16[2,256,2560]{1,2,0:T(8,128)(2,1)}, u32[]{:S(2)}, u32[]{:S(2)}) %collective-permute-start) | collective-permute-done | bytes 2621472 | tf_op jit(solution)/shard_map/ppermute | solution.py:16
  678.5 3.3 pad_maximum_fusion
  681.8 0.0 copy-start.2
  681.8 3.4 fusion.15
  685.3 0.0 copy-done.2
  685.3 10.6 %fusion.16 = (f32[20,256]{1,0:T(8,128)S(1)}, f32[20,256,768]{1,2,0:T(8,128)}) fusion(pred[768]{0:T(1024)(128)(4,1)S(1)} %pad_add_fusion, bf16[768,20,128]{0,2,1:T(8,128)(2,1)} %bitcast.32, bf16[256,20,128]{0,2,1:T(8,128)(2,1)S(1)} %bitcast.34), kind=kOutput, calls=%fused_computation.21 | convolution fusion | flops 1022362368 | bytes 20992768 | tf_op jit(solution)/shard_map/sub | solution.py:30
  695.9 0.0 copy-start
  695.9 9.2 %fusion.10 = bf16[20,128,256]{2,1,0:T(8,128)(2,1)} fusion(bf16[768,20,128]{0,2,1:T(8,128)(2,1)} %bitcast.31, f32[20,256,768]{1,2,0:T(8,128)} %get-tuple-element.8, f32[20,256]{1,0:T(8,128)S(1)} %get-tuple-element.7), kind=kOutput, calls=%fused_computation.15 | convolution fusion | flops 1015152640 | bytes 20992000 | tf_op jit(solution)/shard_map/hqk,khd->qhd/dot_general | solution.py:32
  705.1 0.0 all-to-all-done
  705.1 0.0 copy-done
  705.1 13.5 %fusion.9 = bf16[256,5120]{1,0:T(8,128)(2,1)} fusion(bf16[256,2560]{0,1:T(8,128)(2,1)} %bitcast.33, bf16[2560,5120]{1,0:T(8,128)(2,1)} %bitcast.8, bf16[256,5120]{1,0:T(8,128)(2,1)S(1)} %copy-done), kind=kOutput, calls=%fused_computation.13 | convolution fusion | flops 6714818560 | bytes 32768000 | tf_op jit(solution)/shard_map/dot_general | solution.py:49
  (4 shorter events, 0.0 us)
Async XLA Ops:
  9.7 7.9 %copy-start.1 = (bf16[256,2560]{1,0:T(8,128)(2,1)S(1)}, bf16[256,2560]{1,0:T(8,128)(2,1)}, u32[]{:S(2)}) copy-start(bf16[256,2560]{1,0:T(8,128)(2,1)} %param.6) | copy-start | bytes 3932164
  9.7 695.4 %all-to-all-start = ((bf16[16,160,5120]{2,1,0:T(8,128)(2,1)}), bf16[16,160,5120]{2,1,0:T(8,128)(2,1)}, u32[]{:S(2)}, u32[]{:S(2)}) async-start(bf16[16,160,5120]{2,1,0:T(8,128)(2,1)} %stack.11), calls=%async_computation | async-start | bytes 52428800 | tf_op jit(solution)/shard_map/all_to_all | solution.py:9
  21.6 633.9 %collective-permute-start.1 = (bf16[2,256,2560]{1,2,0:T(8,128)(2,1)}, bf16[2,256,2560]{1,2,0:T(8,128)(2,1)}, u32[]{:S(2)}, u32[]{:S(2)}) collective-permute-start(bf16[2,256,2560]{1,2,0:T(8,128)(2,1)} %pad_maximum_fusion.1), channel_id=1, source_target_pairs={{1,0},{2,1},{3,2},{4,3},{5,4},{6,5},{7,6},{8,7},{9,8},{10,9},{11,1... | collective-permute-start | bytes 7864328 | tf_op jit(solution)/shard_map/ppermute | solution.py:16
  25.8 652.7 %collective-permute-start = (bf16[2,256,2560]{1,2,0:T(8,128)(2,1)}, bf16[2,256,2560]{1,2,0:T(8,128)(2,1)}, u32[]{:S(2)}, u32[]{:S(2)}) collective-permute-start(bf16[2,256,2560]{1,2,0:T(8,128)(2,1)} %pad_maximum_fusion.1), channel_id=1, source_target_pairs={{0,1},{1,2},{2,3},{3,4},{4,5},{5,6},{6,7},{7,8},{8,9},{9,10},{10,1... | collective-permute-start | bytes 7864328 | tf_op jit(solution)/shard_map/ppermute | solution.py:16
  681.8 3.4 copy-start.2
  695.9 9.2 %copy-start = (bf16[256,5120]{1,0:T(8,128)(2,1)S(1)}, bf16[256,5120]{1,0:T(8,128)(2,1)}, u32[]{:S(2)}) copy-start(bf16[256,5120]{1,0:T(8,128)(2,1)} %param.8) | copy-start | bytes 7864324
